TPU v7x, 32 devices: a whole 2x2x4 slice. The times are simulated.
32 devices in a mesh: orient: 4 (over z), dom: 2 (over core), shell: 4 (over y, x).
Axes of the slice: x: 2, y: 2, z: 4, core: 2. Of those that a mesh axis runs over, the one named last changes fastest.
Arguments:
- references: bfloat16 [2048, 2, 4096], P('orient', None, 'shell'), may hold values from -6 to 6
- images: bfloat16 [512, 2, 4096], P(('orient', 'dom'), None, 'shell'), may hold values from -20 to 20
- noise_var: float32 [64], replicated, may hold values from 32 to 128
- shell_of: int32 [4096], P('shell'), may hold values from 0 to 63, never falling along the last dimension, each value on 1 to 128 neighbouring positions
- kept_blocks: int32 [4, 2, 3], P('orient', 'dom'), may hold values from -1 to 3, as said below
Outputs:
- weighted: float32 [2048, 2, 4096], P(('orient', 'dom'), None, 'shell')
- log_norm: float32 [512], P(('orient', 'dom'))
Inputs may be any that keep to these rules, and one draw needn't show every extreme that they name: `kept_blocks`: each list holds distinct block numbers first, then -1 entries; the list of orientation block o and group d always starts with o; some list holds 3 blocks.
All inputs are finite; a program needn't handle non-finite values.
Results may differ from a plain program's by a relative error of at most 0.0051.
Values may be sent and summed in bfloat16 or wider, within the bound.
A program may use at most 64 MiB of HBM per device.

v0:
```python
import functools

import jax
import jax.numpy as jnp
from jax import lax
from jax.experimental import pallas as pl
from jax.experimental.pallas import tpu as pltpu
from jax.sharding import PartitionSpec as P

floor_value = -1e30
MESH = pl.DeviceIdType.MESH


def kernel(
    sizes, kept_ref, noise_ref, shell_ref, raw_ref, whole_ref, prob_ref, home_ref, keep_ref,
    images, part, accum, logn_ref, refs_ref, turned, stage, img_stage, flat_ref, recvp, ebuf, abuf, erecv, lstat, zstat, w_s, rn_s,
    up_sem, dn_sem, img_sem, dom_send, dom_recv, rs_send, rs_recv,
    st_send, st_recv, e_send, e_recv, z_send, z_recv, out_sem, raw_sem, own_sem,
):
    O, D, S = sizes
    z, d, s = lax.axis_index("orient"), lax.axis_index("dom"), lax.axis_index("shell")
    rows, _, half = raw_ref.shape
    img_rows = whole_ref.shape[0]
    lanes = rows // S
    per = S // D
    most = kept_ref.shape[0]
    owner = s // per
    slot = s % per

    def dev(a, b, c):
        return {"orient": a, "dom": b, "shell": c}

    own = pltpu.make_async_copy(whole_ref, img_stage, own_sem)
    own.start()
    fetch = pltpu.make_async_copy(raw_ref, stage, raw_sem)
    fetch.start()
    barrier = pltpu.get_barrier_semaphore()
    for ok, to in ((z < O - 1, z + 1), (z > 0, z + O - 1)):
        @pl.when(ok)
        def _():
            pl.semaphore_signal(
                barrier, inc=1, device_id=dev(lax.rem(to, O), d, s), device_id_type=MESH)

    for od in range(D):
        for os in range(S):
            if od or os:
                pl.semaphore_signal(
                    barrier, inc=1,
                    device_id=dev(z, lax.rem(d + od, D), lax.rem(s + os, S)),
                    device_id_type=MESH,
                )
    own.wait()
    x = img_stage[...]
    for c in range(2):
        flat_ref[:, c * half:(c + 1) * half] = x[:, c, :]

    def img_ref(c):
        return flat_ref.at[:, c * half:(c + 1) * half]

    near = jnp.where(z < O - 1, 1, 0) + jnp.where(z > 0, 1, 0)
    pl.semaphore_wait(barrier, near + D * S - 1)

    def halves(b, j):
        return lambda c: images.at[b, j, c]

    def up(src, j, c):
        return pltpu.make_async_remote_copy(
            src_ref=src(c), dst_ref=images.at[d, j, c], send_sem=up_sem.at[j, c],
            recv_sem=img_sem.at[j, c],
            device_id=dev(lax.rem(z + 1, O), d, s), device_id_type=MESH)

    def down(src, j, c):
        return pltpu.make_async_remote_copy(
            src_ref=src(c), dst_ref=images.at[d, j, c], send_sem=dn_sem.at[j, c],
            recv_sem=img_sem.at[j, c],
            device_id=dev(lax.rem(z + O - 1, O), d, s), device_id_type=MESH)

    def across(src, od, j, c):
        return pltpu.make_async_remote_copy(
            src_ref=src(c), dst_ref=images.at[d, j, c], send_sem=dom_send.at[od, j, c],
            recv_sem=dom_recv.at[od, j, c],
            device_id=dev(z, lax.rem(d + od, D), s), device_id_type=MESH)

    def scatter(j, o):
        to = lax.rem(s + o, S)
        return pltpu.make_async_remote_copy(
            src_ref=part.at[j, to], dst_ref=recvp.at[j, o], send_sem=rs_send.at[j, o],
            recv_sem=rs_recv.at[j, o], device_id=dev(z, d, to), device_id_type=MESH)

    @pl.when(z < O - 1)
    def _():
        for c in range(2):
            up(img_ref, z, c).start()

    @pl.when(z > 0)
    def _():
        for c in range(2):
            down(img_ref, z, c).start()

    for od in range(1, D):
        for c in range(2):
            across(img_ref, od, z, c).start()

    def keep_copy(src, b, j, c):
        return pltpu.make_async_copy(src(c), keep_ref.at[c, b, j], out_sem.at[b, j, c])

    for c in range(2):
        keep_copy(img_ref, d, z, c).start()

    shell = shell_ref[...]
    noise = jnp.ones(shell.shape, jnp.float32)
    for i in range(noise_ref.shape[0]):
        noise = jnp.where(shell == i, noise_ref[i], noise)
    w = 1.0 / noise
    w_s[...] = w

    def norm_rows(c, carry):
        r0 = pl.multiple_of(c * lanes, lanes)
        x = stage[pl.ds(r0, lanes)]
        refs_ref[pl.ds(r0, lanes), :half] = x[:, 0, :]
        refs_ref[pl.ds(r0, lanes), half:] = x[:, 1, :]
        x0 = refs_ref[pl.ds(r0, lanes), :half].astype(jnp.float32)
        x1 = refs_ref[pl.ds(r0, lanes), half:].astype(jnp.float32)
        y = (x0 * x0 + x1 * x1) * w_s[...]
        acc = y[:, :128]
        for k in range(1, y.shape[1] // 128):
            acc = acc + y[:, k * 128:(k + 1) * 128]
        rn_s[c] = 0.5 * jnp.sum(acc.T, axis=0, keepdims=True)
        return carry

    fetch.wait()
    lax.fori_loop(0, S, norm_rows, 0)

    def cross(src, c):
        scaled = (src(c)[...].astype(jnp.float32) * w_s[...]).astype(jnp.bfloat16)
        return lax.dot_general(
            scaled, refs_ref[:, c * half:(c + 1) * half], (((1,), (1,)), ((), ())),
            preferred_element_type=jnp.float32)

    def finish(full, j):
        for k in range(S):
            part[j, k] = full[:, k * lanes:(k + 1) * lanes] - rn_s[k]
        for o in range(1, S):
            scatter(j, o).start()

    def own_block():
        finish(cross(img_ref, 0) + cross(img_ref, 1), z)

    if O == 1:
        own_block()

    def arrive(block, j, c, hop, onward):
        hop(block, j, c).wait_recv()

        @pl.when(onward)
        def _():
            hop(block, j, c).start()

        for od in range(1, D):
            across(block, od, j, c).start()
        keep_copy(block, d, j, c).start()

    lane = lax.broadcasted_iota(jnp.int32, (img_rows, lanes), 1)

    def reduce_block(j):
        v = part[j, s]
        for o in range(1, S):
            scatter(j, o).wait_recv()
            v = v + recvp[j, o]
        want = jnp.full((img_rows, lanes), j, jnp.int32)
        keep = want == kept_ref[0]
        for k in range(1, most):
            keep = keep | (want == kept_ref[k])
        v = jnp.where(keep, v, floor_value)
        m = jnp.max(v, axis=1, keepdims=True)
        e = jnp.where(keep, jnp.exp(v - m), 0.0)
        total = jnp.sum(e, axis=1, keepdims=True)
        at = pl.ds(pl.multiple_of(j * img_rows, img_rows), img_rows)
        ebuf[at, :] = e.astype(jnp.bfloat16)
        abuf[at, :] = jnp.where(lane == 0, m, total)

    def step(t, carry):
        lo = z - t
        hi = z + t
        for c in range(2):
            @pl.when(lo >= 0)
            def _():
                arrive(halves(d, lo), lo, c, up, z < O - 1)

            @pl.when(hi < O)
            def _():
                arrive(halves(d, hi), hi, c, down, z > 0)

            if c == 0:
                pl.when(t == 1)(own_block)

            for side, j, ok in ((0, lo, lo >= 0), (1, hi, hi < O)):
                @pl.when(ok)
                def _():
                    full = cross(halves(d, j), c)
                    if c == 0:
                        accum[side] = full
                    else:
                        finish(accum[side] + full, j)

            if c == 1:
                @pl.when(lo + 1 >= 0)
                def _():
                    reduce_block(lo + 1)

                @pl.when((hi - 1 < O) & (t > 1))
                def _():
                    reduce_block(hi - 1)

        return carry

    lax.fori_loop(1, O, step, 0)

    @pl.when(z == O - 1)
    def _():
        reduce_block(0)

    @pl.when(z == 0)
    def _():
        reduce_block(O - 1)


    lstat[d, s] = abuf[...].T[:2, :]

    def spread(od, os):
        return pltpu.make_async_remote_copy(
            src_ref=lstat.at[d, s], dst_ref=lstat.at[d, s], send_sem=st_send.at[od, os],
            recv_sem=st_recv.at[od, os],
            device_id=dev(z, lax.rem(d + od, D), lax.rem(s + os, S)), device_id_type=MESH)

    peers = [(od, os) for od in range(D) for os in range(S) if od or os]
    for od, os in peers:
        spread(od, os).start()

    def give(to):
        return pltpu.make_async_remote_copy(
            src_ref=ebuf, dst_ref=erecv.at[d, slot], send_sem=e_send.at[to],
            recv_sem=e_recv.at[d, slot], device_id=dev(z, owner, to), device_id_type=MESH)

    def each_give(act):
        for to in range(S):
            @pl.when((owner != d) | (s != to))
            def _():
                act(give(to))

    each_give(lambda c: c.start())

    @pl.when(owner == d)
    def _():
        erecv[d, slot] = ebuf[...]

    for od, os in peers:
        spread(od, os).wait_recv()
    for b in range(D):
        m = lstat[b, 0, 0:1, :]
        for k in range(1, S):
            m = jnp.maximum(m, lstat[b, k, 0:1, :])
        total = jnp.zeros_like(m)
        for k in range(S):
            total = total + lstat[b, k, 1:2, :] * jnp.exp(lstat[b, k, 0:1, :] - m)
        zstat[z, b, 0:1, :] = m
        zstat[z, b, 1:2, :] = total

    def column(o):
        return pltpu.make_async_remote_copy(
            src_ref=zstat.at[z], dst_ref=zstat.at[z], send_sem=z_send.at[o], recv_sem=z_recv.at[o],
            device_id=dev(lax.rem(z + o, O), d, s), device_id_type=MESH)

    for o in range(1, O):
        column(o).start()
    def dom_wait(j, carry):
        for od in range(1, D):
            b = lax.rem(d + D - od, D)
            for c in range(2):
                across(halves(d, j), od, j, c).wait_recv()
                keep_copy(halves(b, j), b, j, c).start()
        return carry

    lax.fori_loop(0, O, dom_wait, 0)

    for q in range(per):
        for b in range(D):
            @pl.when((d * per + q != s) | (d != b))
            def _():
                pltpu.make_async_remote_copy(
                    src_ref=ebuf, dst_ref=erecv.at[b, q], send_sem=e_send.at[0],
                    recv_sem=e_recv.at[b, q], device_id=dev(z, lax.rem(d + 1, D), s),
                    device_id_type=MESH).wait_recv()
    for q in range(per):
        for b in range(D):
            turned[b, q] = erecv[b, q].astype(jnp.float32).T

    for o in range(1, O):
        column(o).wait_recv()
    for b in range(D):
        m = zstat[0, b, 0:1, :]
        for k in range(1, O):
            m = jnp.maximum(m, zstat[k, b, 0:1, :])
        total = jnp.zeros_like(m)
        for k in range(O):
            total = total + zstat[k, b, 1:2, :] * jnp.exp(zstat[k, b, 0:1, :] - m)
        logn_ref[b:b + 1, :] = m + jnp.log(total)

    home = logn_ref[pl.ds(d, 1), :]
    pick = home[:, :img_rows]
    for j in range(1, O):
        pick = jnp.where(z == j, home[:, j * img_rows:(j + 1) * img_rows], pick)
    home_ref[...] = pick


    depth = O * img_rows
    for q in range(per):
        for b in range(D):
            scale = jnp.exp(lstat[b, d * per + q, 0:1, :] - logn_ref[b:b + 1, :])
            p = (turned[b, q] * scale).astype(jnp.bfloat16)
            prob_ref[q * lanes:(q + 1) * lanes, b * depth:(b + 1) * depth] = p

    @pl.when(z < O - 1)
    def _():
        def done(j, carry):
            @pl.when(j <= z)
            def _():
                for c in range(2):
                    up(img_ref, j, c).wait_send()
            return carry
        lax.fori_loop(0, O, done, 0)

    @pl.when(z > 0)
    def _():
        def done(j, carry):
            @pl.when(j >= z)
            def _():
                for c in range(2):
                    down(img_ref, j, c).wait_send()
            return carry
        lax.fori_loop(0, O, done, 0)

    def sent(j, carry):
        for od in range(1, D):
            for c in range(2):
                across(img_ref, od, j, c).wait_send()
        for b in range(D):
            for c in range(2):
                keep_copy(img_ref, b, j, c).wait()
        for o in range(1, S):
            scatter(j, o).wait_send()
        return carry

    lax.fori_loop(0, O, sent, 0)
    for od, os in peers:
        spread(od, os).wait_send()
    each_give(lambda c: c.wait_send())
    for o in range(1, O):
        column(o).wait_send()


def product(prob_ref, home_ref, keep_ref, out_ref, logn_ref, images, total, in_sem, out_sem):
    halves, width, wide = 2, images.shape[2], 512

    def fetch(c, n):
        cols = pl.ds(n * wide, wide)
        return pltpu.make_async_copy(
            keep_ref.at[c, :, cols], images.at[c, :, cols], in_sem.at[c, n])

    def put(c, n):
        cols = pl.ds(n * wide, wide)
        return pltpu.make_async_copy(
            total.at[c, :, cols], out_ref.at[:, c, cols], out_sem.at[c, n])

    for c in range(halves):
        for n in range(width // wide):
            fetch(c, n).start()
    logn_ref[...] = home_ref[...]
    for c in range(halves):
        for n in range(width // wide):
            fetch(c, n).wait()
            cols = slice(n * wide, (n + 1) * wide)
            total[c, :, cols] = jnp.dot(
                prob_ref[...], images[c, :, cols], preferred_element_type=jnp.float32)
            put(c, n).start()
    for c in range(halves):
        for n in range(width // wide):
            put(c, n).wait()


def shards(references, images, noise_var, shell_of, kept_blocks):
    O, D, S = (lax.axis_size(a) for a in ("orient", "dom", "shell"))
    rows = references.shape[0]
    img_rows = images.shape[0]
    local = references.shape[2]
    flat = 2 * local
    lanes = rows // S
    own = rows // D
    columns = O * img_rows
    vmem = pl.BlockSpec(memory_space=pltpu.VMEM)
    smem = pl.BlockSpec(memory_space=pltpu.SMEM)
    sem = pltpu.SemaphoreType.DMA
    f32, bf16 = jnp.float32, jnp.bfloat16
    probs, home, kept_images = pl.pallas_call(
        functools.partial(kernel, (O, D, S)),
        name="expectation",
        out_shape=(
            jax.ShapeDtypeStruct((own, D * columns), bf16),
            jax.ShapeDtypeStruct((1, img_rows), f32),
            jax.ShapeDtypeStruct((2, D, O, img_rows, local), bf16),
        ),
        in_specs=[smem, smem, vmem, pl.BlockSpec(memory_space=pl.ANY), pl.BlockSpec(memory_space=pl.ANY)],
        out_specs=(vmem, vmem, pl.BlockSpec(memory_space=pl.ANY)),
        scratch_shapes=[
            pltpu.VMEM((D, O, 2, img_rows, local), bf16),
            pltpu.VMEM((O, S, img_rows, lanes), f32),
            pltpu.VMEM((2, img_rows, rows), f32),
            pltpu.VMEM((D, columns), f32),
            pltpu.VMEM((rows, flat), bf16),
            pltpu.VMEM((D, S // D, lanes, columns), f32),
            pltpu.VMEM((rows, 2, local), bf16),
            pltpu.VMEM((img_rows, 2, local), bf16),
            pltpu.VMEM((img_rows, flat), bf16),
            pltpu.VMEM((O, S, img_rows, lanes), f32),
            pltpu.VMEM((columns, lanes), bf16),
            pltpu.VMEM((columns, lanes), f32),
            pltpu.VMEM((D, S // D, columns, lanes), bf16),
            pltpu.VMEM((D, S, 2, columns), f32),
            pltpu.VMEM((O, D, 2, columns), f32),
            pltpu.VMEM((1, local), f32),
            pltpu.VMEM((S, 1, lanes), f32),
            sem((O, 2)), sem((O, 2)), sem((O, 2)),
            sem((D, O, 2)), sem((D, O, 2)),
            sem((O, S)), sem((O, S)),
            sem((D, S)), sem((D, S)),
            sem((S,)), sem((D, S // D)),
            sem((O,)), sem((O,)), sem((D, O, 2)), sem, sem,
        ],
        compiler_params=pltpu.CompilerParams(collective_id=0, has_side_effects=True),
    )(
        kept_blocks.reshape(-1),
        noise_var,
        shell_of.reshape(1, -1),
        references,
        images,
    )
    depth = D * columns
    weighted, log_norm = pl.pallas_call(
        product,
        name="product",
        out_shape=(
            jax.ShapeDtypeStruct((own, 2, local), f32),
            jax.ShapeDtypeStruct((1, img_rows), f32),
        ),
        in_specs=[vmem, vmem, pl.BlockSpec(memory_space=pl.ANY)],
        out_specs=(pl.BlockSpec(memory_space=pl.ANY), vmem),
        scratch_shapes=[
            pltpu.VMEM((2, depth, local), bf16),
            pltpu.VMEM((2, own, local), f32),
            sem((2, local // 512)),
            sem((2, local // 512)),
        ],
    )(probs, home, kept_images.reshape(2, depth, local))
    return weighted, log_norm.reshape(img_rows)


def solution(mesh):
    placed = (
        P("orient", None, "shell"),
        P(("orient", "dom"), None, "shell"),
        P(),
        P("shell"),
        P("orient", "dom", None),
    )
    return jax.shard_map(
        shards,
        mesh=mesh,
        in_specs=placed,
        out_specs=(P(("orient", "dom"), None, "shell"), P(("orient", "dom"))),
        check_vma=False,
    )
```

profile of v0, /device:TPU:0, one launch (start us, length us, event | category | flops | bytes accessed | tf_op | source)
XLA Modules:
  0.0 43.1 jit_solution(1812460219911504131)
XLA Ops:
  0.6 37.9 %expectation.1 = (bf16[256,512]{1,0:T(8,128)(2,1)}, f32[1,64]{1,0:T(1,128)}, bf16[2,2,4,64,1024]{4,3,2,1,0:T(8,128)(2,1)}) custom-call(s32[3]{0:T(128)} %bitcast.6, f32[64]{0:T(128)} %noise_ref.1, s32[1,1024]{1,0:T(1,128)} %bitcast.5, bf16[512,2,1024]{2,1,0:T(2,128)(2,1)} %raw_ref.1, bf16[64,2,1024]{2,1,0:T(2,128)(2,1)} %whole_ref.1), custom_call_target="tpu_custom_call" | custom-call | tf_op jit(solution)/shard_map/expectation/pallas_call | solution.py:404
  38.5 4.6 %product.1 = (f32[256,2,1024]{2,1,0:T(2,128)}, f32[1,64]{1,0:T(1,128)}) custom-call(bf16[256,512]{1,0:T(8,128)(2,1)} %get-tuple-element.7.prob_ref, f32[1,64]{1,0:T(1,128)} %get-tuple-element.8.home_ref, bf16[2,512,1024]{2,1,0:T(8,128)(2,1)} %bitcast.4), custom_call_target="tpu_custom_call" | custom-call | tf_op jit(solution)/shard_map/product/pallas_call | solution.py:448
where the time goes:
time: 43.3 us; the launch traced here: 43.1 us
  Pallas kernels  42.5 us (98%)
  between operations  0.64 us (1%)
    pallas_call x1, Pallas kernels, shards(): pl.pallas_call(functools.partial(kernel, (O, D, S)), name='expectation',...  37.9 us
    pallas_call x1, Pallas kernels, shards(): pl.pallas_call(product, name='product', out_shape=(jax.ShapeDtypeStruct((...  4.59 us

commit v1 on v0

--- a/solution.py
+++ b/solution.py
@@ -1,4 +1,5 @@
 import functools
+import math
 
 import jax
 import jax.numpy as jnp
@@ -359,26 +360,17 @@
         column(o).wait_send()
 
 
-def product(prob_ref, home_ref, keep_ref, out_ref, logn_ref, images, total, in_sem, out_sem):
+def product(prob_ref, home_ref, images, out_ref, logn_ref, total, out_sem):
     halves, width, wide = 2, images.shape[2], 512
-
-    def fetch(c, n):
-        cols = pl.ds(n * wide, wide)
-        return pltpu.make_async_copy(
-            keep_ref.at[c, :, cols], images.at[c, :, cols], in_sem.at[c, n])
 
     def put(c, n):
         cols = pl.ds(n * wide, wide)
         return pltpu.make_async_copy(
             total.at[c, :, cols], out_ref.at[:, c, cols], out_sem.at[c, n])
 
-    for c in range(halves):
-        for n in range(width // wide):
-            fetch(c, n).start()
     logn_ref[...] = home_ref[...]
     for c in range(halves):
         for n in range(width // wide):
-            fetch(c, n).wait()
             cols = slice(n * wide, (n + 1) * wide)
             total[c, :, cols] = jnp.dot(
                 prob_ref[...], images[c, :, cols], preferred_element_type=jnp.float32)
@@ -386,6 +378,14 @@
     for c in range(halves):
         for n in range(width // wide):
             put(c, n).wait()
+
+
+def grant(shapes):
+    total = 4 * 1024 * 1024
+    for item in shapes:
+        if getattr(item, "memory_space", None) == pltpu.VMEM:
+            total += math.prod(item.shape) * jnp.dtype(item.dtype).itemsize
+    return total
 
 
 def shards(references, images, noise_var, shell_of, kept_blocks):
@@ -401,6 +401,31 @@
     smem = pl.BlockSpec(memory_space=pltpu.SMEM)
     sem = pltpu.SemaphoreType.DMA
     f32, bf16 = jnp.float32, jnp.bfloat16
+    first = [
+        pltpu.VMEM((D, O, 2, img_rows, local), bf16),
+        pltpu.VMEM((O, S, img_rows, lanes), f32),
+        pltpu.VMEM((2, img_rows, rows), f32),
+        pltpu.VMEM((D, columns), f32),
+        pltpu.VMEM((rows, flat), bf16),
+        pltpu.VMEM((D, S // D, lanes, columns), f32),
+        pltpu.VMEM((rows, 2, local), bf16),
+        pltpu.VMEM((img_rows, 2, local), bf16),
+        pltpu.VMEM((img_rows, flat), bf16),
+        pltpu.VMEM((O, S, img_rows, lanes), f32),
+        pltpu.VMEM((columns, lanes), bf16),
+        pltpu.VMEM((columns, lanes), f32),
+        pltpu.VMEM((D, S // D, columns, lanes), bf16),
+        pltpu.VMEM((D, S, 2, columns), f32),
+        pltpu.VMEM((O, D, 2, columns), f32),
+        pltpu.VMEM((1, local), f32),
+        pltpu.VMEM((S, 1, lanes), f32),
+        sem((O, 2)), sem((O, 2)), sem((O, 2)),
+        sem((D, O, 2)), sem((D, O, 2)),
+        sem((O, S)), sem((O, S)),
+        sem((D, S)), sem((D, S)),
+        sem((S,)), sem((D, S // D)),
+        sem((O,)), sem((O,)), sem((D, O, 2)), sem, sem,
+    ]
     probs, home, kept_images = pl.pallas_call(
         functools.partial(kernel, (O, D, S)),
         name="expectation",
@@ -409,42 +434,22 @@
             jax.ShapeDtypeStruct((1, img_rows), f32),
             jax.ShapeDtypeStruct((2, D, O, img_rows, local), bf16),
         ),
-        in_specs=[smem, smem, vmem, pl.BlockSpec(memory_space=pl.ANY), pl.BlockSpec(memory_space=pl.ANY)],
+        in_specs=[smem, smem, vmem, pl.BlockSpec(memory_space=pltpu.HBM), pl.BlockSpec(memory_space=pltpu.HBM)],
         out_specs=(vmem, vmem, pl.BlockSpec(memory_space=pl.ANY)),
-        scratch_shapes=[
-            pltpu.VMEM((D, O, 2, img_rows, local), bf16),
-            pltpu.VMEM((O, S, img_rows, lanes), f32),
-            pltpu.VMEM((2, img_rows, rows), f32),
-            pltpu.VMEM((D, columns), f32),
-            pltpu.VMEM((rows, flat), bf16),
-            pltpu.VMEM((D, S // D, lanes, columns), f32),
-            pltpu.VMEM((rows, 2, local), bf16),
-            pltpu.VMEM((img_rows, 2, local), bf16),
-            pltpu.VMEM((img_rows, flat), bf16),
-            pltpu.VMEM((O, S, img_rows, lanes), f32),
-            pltpu.VMEM((columns, lanes), bf16),
-            pltpu.VMEM((columns, lanes), f32),
-            pltpu.VMEM((D, S // D, columns, lanes), bf16),
-            pltpu.VMEM((D, S, 2, columns), f32),
-            pltpu.VMEM((O, D, 2, columns), f32),
-            pltpu.VMEM((1, local), f32),
-            pltpu.VMEM((S, 1, lanes), f32),
-            sem((O, 2)), sem((O, 2)), sem((O, 2)),
-            sem((D, O, 2)), sem((D, O, 2)),
-            sem((O, S)), sem((O, S)),
-            sem((D, S)), sem((D, S)),
-            sem((S,)), sem((D, S // D)),
-            sem((O,)), sem((O,)), sem((D, O, 2)), sem, sem,
-        ],
-        compiler_params=pltpu.CompilerParams(collective_id=0, has_side_effects=True),
+        scratch_shapes=first,
+        compiler_params=pltpu.CompilerParams(collective_id=0, has_side_effects=True, vmem_limit_bytes=grant(first)),
     )(
-        kept_blocks.reshape(-1),
-        noise_var,
-        shell_of.reshape(1, -1),
-        references,
-        images,
+        pltpu.with_memory_space_constraint(kept_blocks.reshape(-1), pltpu.HBM),
+        pltpu.with_memory_space_constraint(noise_var, pltpu.HBM),
+        pltpu.with_memory_space_constraint(shell_of.reshape(1,-1), pltpu.HBM),
+        pltpu.with_memory_space_constraint(references, pltpu.HBM),
+        pltpu.with_memory_space_constraint(images, pltpu.HBM),
     )
     depth = D * columns
+    second = [
+        pltpu.VMEM((2, own, local), f32),
+        sem((2, local // 512)),
+    ]
     weighted, log_norm = pl.pallas_call(
         product,
         name="product",
@@ -452,14 +457,10 @@
             jax.ShapeDtypeStruct((own, 2, local), f32),
             jax.ShapeDtypeStruct((1, img_rows), f32),
         ),
-        in_specs=[vmem, vmem, pl.BlockSpec(memory_space=pl.ANY)],
+        in_specs=[vmem, vmem, vmem],
         out_specs=(pl.BlockSpec(memory_space=pl.ANY), vmem),
-        scratch_shapes=[
-            pltpu.VMEM((2, depth, local), bf16),
-            pltpu.VMEM((2, own, local), f32),
-            sem((2, local // 512)),
-            sem((2, local // 512)),
-        ],
+        scratch_shapes=second,
+        compiler_params=pltpu.CompilerParams(vmem_limit_bytes=grant(second)),
     )(probs, home, kept_images.reshape(2, depth, local))
     return weighted, log_norm.reshape(img_rows)
 

time: 43.3 us -> 40.7 us (0.940)
  Pallas kernels: 42.5 us -> 39.8 us
    pallas_call x1, Pallas kernels: 4.59 us -> 2.58 us  [shards(): pl.pallas_call(product, name='product', out_shape=(jax.ShapeDtypeStruct((...]
    pallas_call x1, Pallas kernels: 37.9 us -> 37.3 us  [shards(): pl.pallas_call(functools.partial(kernel, (O, D, S)), name='expectation',...]
where the time goes in v1:
time: 40.7 us; the launch traced here: 40.5 us
  Pallas kernels  39.8 us (98%)
  between operations  0.64 us (2%)
    pallas_call x1, Pallas kernels, shards(): pl.pallas_call(functools.partial(kernel, (O, D, S)), name='expectation',...  37.3 us
    pallas_call x1, Pallas kernels, shards(): pl.pallas_call(product, name='product', out_shape=(jax.ShapeDtypeStruct((...  2.58 us

profile of v1, /device:TPU:0, one launch (start us, length us, event | category | flops | bytes accessed | tf_op | source)
XLA Modules:
  0.0 40.5 jit_solution(9738643100720706300)
XLA Ops:
  0.6 37.3 %expectation.1 = (bf16[256,512]{1,0:T(8,128)(2,1)S(1)}, f32[1,64]{1,0:T(1,128)S(1)}, bf16[2,2,4,64,1024]{4,3,2,1,0:T(8,128)(2,1)S(1)}) custom-call(s32[3]{0:T(128)} %bitcast.6, f32[64]{0:T(128)} %noise_ref.1, s32[1,1024]{1,0:T(1,128)} %bitcast.5, bf16[512,2,1024]{2,1,0:T(2,128)(2,1)} %raw_ref.1, bf16[64,2,1024]{2,1,0:T(2,128)(2,1)} %whole_ref.1), custom_call_target="tpu_custom_call" | custom-call | tf_op jit(solution)/shard_map/expectation/pallas_call | solution.py:429
  37.9 2.6 %product.1 = (f32[256,2,1024]{2,1,0:T(2,128)}, f32[1,64]{1,0:T(1,128)}) custom-call(bf16[256,512]{1,0:T(8,128)(2,1)S(1)} %get-tuple-element.7.prob_ref, f32[1,64]{1,0:T(1,128)S(1)} %get-tuple-element.8.home_ref, bf16[2,512,1024]{2,1,0:T(8,128)(2,1)S(1)} %bitcast.4), custom_call_target="tpu_custom_call" | custom-call | tf_op jit(solution)/shard_map/product/pallas_call | solution.py:453

commit v2 on v1

v2 whole, which is shorter than its diff:
```python
import functools
import math

import jax
import jax.numpy as jnp
from jax import lax
from jax.experimental import pallas as pl
from jax.experimental.pallas import tpu as pltpu
from jax.sharding import PartitionSpec as P

floor_value = -1e30
MESH = pl.DeviceIdType.MESH
ahead = 2


def kernel(
    sizes, kept_hbm, noise_hbm, shell_hbm, raw_ref, whole_ref, prob_ref, home_ref, keep_ref,
    images, slots, kout, kin, shift, part, recvp, held, refs_ref, stage, img_stage,
    ebuf, erecv, lstat, zstat, logn, w_s, rn_s, shell_ref, kept_ref, noise_ref, ids,
    up_sem, dn_sem, img_sem, dom_send, dom_recv, rs_send, rs_recv, st_send, st_recv,
    e_send, e_recv, z_send, z_recv, k_send, k_recv, out_sem, in_sem,
):
    O, D, S = sizes
    z, d, s = lax.axis_index("orient"), lax.axis_index("dom"), lax.axis_index("shell")
    rows, _, half = raw_ref.shape
    img_rows = whole_ref.shape[0]
    lanes = rows // S
    per = S // D
    most = kept_ref.shape[0]
    owner = s // per
    slot = s % per
    skip = max(O - most, 0)
    room = O - 1 - skip
    hops = max(O - 2, room)
    pieces, chunks = 8, 8
    hr, qr, pr = img_rows // 2, img_rows // 4, rows // pieces

    def dev(a, b, c):
        return {"orient": a, "dom": b, "shell": c}

    inputs = [
        pltpu.make_async_copy(src, dst, in_sem.at[i])
        for i, (src, dst) in enumerate((
            (whole_ref, img_stage), (raw_ref, stage), (kept_hbm, kept_ref),
            (noise_hbm, noise_ref), (shell_hbm, shell_ref)))
    ]
    for copy in inputs:
        copy.start()
    barrier = pltpu.get_barrier_semaphore()
    for ok, to in ((z < O - 1, z + 1), (z > 0, z + O - 1)):
        @pl.when(ok)
        def _():
            pl.semaphore_signal(
                barrier, inc=1, device_id=dev(lax.rem(to, O), d, s), device_id_type=MESH)

    for od in range(D):
        for os in range(S):
            if od or os:
                pl.semaphore_signal(
                    barrier, inc=1,
                    device_id=dev(z, lax.rem(d + od, D), lax.rem(s + os, S)),
                    device_id_type=MESH,
                )

    def used(p):
        if not skip:
            return p >= 0
        return jnp.logical_not(((z == O - 1) & (p < skip)) | ((z == 0) & (p > room)))

    def has(side, t):
        p = z - t if side == 0 else z + t
        inside = (p >= 0) & (p < O)
        return inside & used(p)

    def on(t, act):
        if isinstance(t, int) and t == 0:
            act(z, 0)
            return
        for side in range(2):
            @pl.when(has(side, t))
            def _():
                act(z - t if side == 0 else z + t, side)

    def piece(n):
        h, c, q = n // 4, (n // 2) % 2, n % 2
        return c, pl.ds(h * hr + q * qr, qr)

    def hop(side, src, p, n):
        c, at = piece(n)
        to = lax.rem(z + 1, O) if side == 0 else lax.rem(z + O - 1, O)
        send = up_sem if side == 0 else dn_sem
        return pltpu.make_async_remote_copy(
            src_ref=src.at[c, at], dst_ref=images.at[d, p, c, at], send_sem=send.at[p],
            recv_sem=img_sem.at[p, n], device_id=dev(to, d, s), device_id_type=MESH)

    def step(side, p, m):
        return p - m if side == 0 else p + m

    def choose(side, k, n):
        c, at = piece(n)
        first = step(side, z, k)
        v = images[d, first, c, at].astype(jnp.float32)
        for m in range(1, skip + 1):
            other = images[d, step(side, first, m), c, at].astype(jnp.float32)
            v = jnp.where(shift[side, k + m] == m, other, v)
        slots[side, k, c, at] = v.astype(jnp.bfloat16)

    def relay(side, t, n):
        p = step(side, z, t)
        edge = O - 1 if side == 0 else 0
        before = O - 2 if side == 0 else 1
        plain = (z != edge) & (z != before) if skip else z != edge

        @pl.when(plain)
        def _():
            hop(side, images.at[d, p], p, n).start()

        if skip and not (isinstance(t, int) and t < skip):
            k = t - skip

            @pl.when((z == before) & (k >= 0) & (k < room))
            def _():
                choose(side, k, n)
                hop(side, slots.at[side, k], step(side, z, k), n).start()

    def serve(t, n):
        def arrived(p, side):
            hop(side, images.at[d, p], p, n).wait_recv()
            relay(side, t, n)
        on(t, arrived)

    def across(od, p):
        return pltpu.make_async_remote_copy(
            src_ref=images.at[d, p], dst_ref=images.at[d, p],
            send_sem=dom_send.at[od - 1, p], recv_sem=dom_recv.at[od - 1, p],
            device_id=dev(z, lax.rem(d + od, D), s), device_id_type=MESH)

    def keep_copy(b, p):
        return pltpu.make_async_copy(images.at[b, p], keep_ref.at[:, b, p], out_sem)

    def landed(p, side):
        for od in range(1, D):
            across(od, p).start()
        keep_copy(d, p).start()

    def scatter(p, h, o):
        to = lax.rem(s + o, S)
        at = pl.ds(h * hr, hr)
        return pltpu.make_async_remote_copy(
            src_ref=part.at[p, to, at], dst_ref=recvp.at[p, o - 1, at], send_sem=rs_send.at[p],
            recv_sem=rs_recv.at[p], device_id=dev(z, d, to), device_id_type=MESH)

    peers = [(od, os) for od in range(D) for os in range(S) if od or os]

    def spread(p, od, os):
        return pltpu.make_async_remote_copy(
            src_ref=lstat.at[d * S + s, p], dst_ref=lstat.at[d * S + s, p],
            send_sem=st_send.at[p], recv_sem=st_recv.at[p],
            device_id=dev(z, lax.rem(d + od, D), lax.rem(s + os, S)), device_id_type=MESH)

    def give(p, to):
        return pltpu.make_async_remote_copy(
            src_ref=ebuf.at[p], dst_ref=erecv.at[d * per + slot, p], send_sem=e_send,
            recv_sem=e_recv, device_id=dev(z, owner, to), device_id_type=MESH)

    def give_all(p, side):
        for to in range(S):
            @pl.when((owner != d) | (s != to))
            def _():
                give(p, to).start()

    def publish(p, m, total, name, e):
        mine = d * S + s
        lstat[mine, p, 0:1, :] = m
        lstat[mine, p, 1:2, :] = total
        lstat[mine, p, 2:3, :] = name
        lstat[mine, p, 3:4, :] = jnp.zeros_like(m)
        ebuf[p] = e
        for od, os in peers:
            spread(p, od, os).start()

        @pl.when(owner == d)
        def _():
            erecv[d * per + slot, p] = e

    def drain(ref, send_sem, recv_sem):
        return pltpu.make_async_remote_copy(
            src_ref=ref, dst_ref=ref, send_sem=send_sem, recv_sem=recv_sem,
            device_id=dev(z, lax.rem(d + 1, D), s), device_id_type=MESH)

    def spread_rows(n):
        r0 = pl.multiple_of(n * pr, pr)
        x = stage[pl.ds(r0, pr)]
        refs_ref[pl.ds(r0, pr), :half] = x[:, 0, :]
        refs_ref[pl.ds(r0, pr), half:] = x[:, 1, :]

    def norm_rows(c):
        at = slice(c * lanes, (c + 1) * lanes)
        x0 = refs_ref[at, :half].astype(jnp.float32)
        x1 = refs_ref[at, half:].astype(jnp.float32)
        y = (x0 * x0 + x1 * x1) * w_s[...]
        acc = y[:, :128]
        for k in range(1, y.shape[1] // 128):
            acc = acc + y[:, k * 128:(k + 1) * 128]
        rn_s[c] = 0.5 * jnp.sum(acc.T, axis=0, keepdims=True)

    def cross(p, c, at):
        scaled = (images[d, p, c, at].astype(jnp.float32) * w_s[...]).astype(jnp.bfloat16)
        return lax.dot_general(
            scaled, refs_ref[:, c * half:(c + 1) * half], (((1,), (1,)), ((), ())),
            preferred_element_type=jnp.float32)

    def finish(full, p, h):
        at = pl.ds(h * hr, hr)
        for k in range(S):
            part[p, k, at] = full[:, k * lanes:(k + 1) * lanes] - rn_s[k]
        for o in range(1, S):
            scatter(p, h, o).start()

    def whole_block(p, side):
        every = slice(0, img_rows)
        full = cross(p, 0, every) + cross(p, 1, every)
        for h in range(2):
            finish(full[h * hr:(h + 1) * hr], p, h)

    def reduce_block(p, side):
        drain(recvp.at[p], rs_send.at[p], rs_recv.at[p]).wait_recv()
        v = part[p, s]
        for o in range(S - 1):
            v = v + recvp[p, o]
        v = v.T
        want = jnp.full(v.shape, ids[p], jnp.int32)
        keep = want == kept_ref[0]
        for k in range(1, most):
            keep = keep | (want == kept_ref[k])
        v = jnp.where(keep, v, floor_value)
        m = jnp.max(v, axis=0, keepdims=True)
        e = jnp.where(keep, jnp.exp(v - m), 0.0)
        total = jnp.sum(e, axis=0, keepdims=True)
        publish(p, m, total, want[:1].astype(jnp.float32), e.astype(jnp.bfloat16))

    inputs[0].wait()
    x = img_stage[...]
    for c in range(2):
        images[d, z, c] = x[:, c, :]
    inputs[2].wait()
    inputs[1].wait()
    for n in range(ahead):
        spread_rows(n)
    near = jnp.where(z < O - 1, 1, 0) + jnp.where(z > 0, 1, 0)
    pl.semaphore_wait(barrier, near + D * S - 1)

    def kept_copy(side):
        to = lax.rem(z + O - 1, O) if side == 0 else lax.rem(z + 1, O)
        return pltpu.make_async_remote_copy(
            src_ref=kout, dst_ref=kin.at[side], send_sem=k_send.at[side],
            recv_sem=k_recv.at[side], device_id=dev(to, d, s), device_id_type=MESH)

    if skip:
        @pl.when((z == 0) | (z == O - 1))
        def _():
            for k in range(most):
                kout[k] = jnp.full((1, half), kept_ref[k], jnp.int32).astype(jnp.float32)
        for side, edge in ((0, O - 1), (1, 0)):
            @pl.when(z == edge)
            def _():
                kept_copy(side).start()

    for n in range(chunks):
        for side in range(2):
            relay(side, 0, n)

    landed(z, 0)

    def candidate(side, c):
        return O - 2 - c if side == 0 else 1 + c

    for p in range(O):
        ids[p] = p
    if skip:
        for side, edge in ((0, O - 1), (1, 0)):
            @pl.when(z == edge)
            def _():
                gone, moved = jnp.int32(0), []
                for c in range(O - 1):
                    moved.append(jnp.minimum(gone, skip))
                    need = kept_ref[0] == candidate(side, c)
                    for k in range(1, most):
                        need = need | (kept_ref[k] == candidate(side, c))
                    gone = gone + jnp.where(need, 0, 1)
                for k in range(room):
                    name = jnp.int32(candidate(side, k))
                    for m in range(1, skip + 1):
                        name = jnp.where(moved[k + m] == m, candidate(side, k + m), name)
                    ids[candidate(side, k)] = name
                for k in range(room, O - 1):
                    p = candidate(side, k)
                    for b in range(D):
                        images[b, p] = jnp.zeros((2, img_rows, half), jnp.bfloat16)
                        keep_copy(b, p).start()
                    publish(
                        p, jnp.full((1, img_rows), floor_value, jnp.float32),
                        jnp.zeros((1, img_rows), jnp.float32),
                        jnp.full((1, img_rows), -2.0, jnp.float32),
                        jnp.zeros((lanes, img_rows), jnp.bfloat16))
                    give_all(p, 0)

    def shifts():
        for side, before in ((0, O - 2), (1, 1)) if skip else ():
            @pl.when(z == before)
            def _():
                kept_copy(side).wait_recv()
                gone = jnp.zeros((1, half), jnp.float32)
                for c in range(O - 1):
                    shift[side, c] = jnp.minimum(gone, skip)
                    need = jnp.zeros((1, half), jnp.float32)
                    for k in range(most):
                        need = jnp.where(kin[side, k] == candidate(side, c), 1.0, need)
                    gone = gone + 1.0 - need

    def weights():
        inputs[3].wait()
        inputs[4].wait()
        shell = shell_ref[...]
        noise = jnp.ones(shell.shape, jnp.float32)
        for i in range(noise_ref.shape[0]):
            noise = jnp.where(shell == i, noise_ref[i], noise)
        w_s[...] = 1.0 / noise

    between = (z > 0) & (z < O - 1)
    edge = jnp.logical_not(between)

    def on_side(side, t, act):
        @pl.when(has(side, t))
        def _():
            act(step(side, z, t), side)

    def reduce_and_give(p, side):
        reduce_block(p, side)
        give_all(p, side)

    def run(t, jobs):
        for n in range(chunks):
            serve(t, n)
            for job in jobs.get(n, ()):
                job()
        on(t, landed)

    @pl.when(edge)
    def _():
        for n in range(ahead, pieces):
            spread_rows(n)
        weights()
        for c in range(S):
            norm_rows(c)
        whole_block(z, 0)
        run(1, {})
        on(1, whole_block)
        reduce_and_give(z, 0)

    @pl.when(between)
    def _():
        for n in range(ahead, ahead + 2):
            spread_rows(n)
        shifts()
        rest = [functools.partial(spread_rows, n) for n in range(ahead + 2, pieces)]
        rest += [weights] + [functools.partial(norm_rows, c) for c in range(S)]
        jobs = {n: [rest[n]] for n in range(4)}
        jobs[4] = rest[4:6]
        jobs[5] = rest[6:]
        jobs[6] = [lambda: whole_block(z, 0)]
        run(1, jobs)

    def middle(t, carry):
        pl.when(edge & (t > 2))(lambda: on(t - 1, whole_block))
        run(t, {
            0: [lambda: pl.when(between)(lambda: on_side(0, t - 1, whole_block))],
            2: [lambda: pl.when(between)(lambda: on_side(1, t - 1, whole_block))],
            4: [lambda: pl.when((t > 2) | between)(lambda: on_side(0, t - 2, reduce_and_give))],
            5: [lambda: pl.when(t > 2)(lambda: on_side(1, t - 2, reduce_and_give))],
        })
        return carry

    lax.fori_loop(2, hops, middle, 0)

    low, high = slice(0, hr), slice(hr, img_rows)

    def first_half(p, side):
        finish(cross(p, 0, low) + cross(p, 1, low), p, 0)

    def third_quarter(p, side):
        held[side] = cross(p, 0, high)

    def last_quarter(p, side):
        finish(held[side] + cross(p, 1, high), p, 1)

    if hops > 2:
        pl.when(edge)(lambda: on(hops - 1, whole_block))
    run(hops, {
        0: [lambda: pl.when(between)(lambda: on_side(0, hops - 1, whole_block))],
        2: [lambda: pl.when(between)(lambda: on_side(1, hops - 1, whole_block))],
        3: [lambda: on(hops, first_half)],
        5: [lambda: on(hops, third_quarter)],
        7: [lambda: on(hops, last_quarter)],
    })
    pl.when(between if hops == 2 else z >= 0)(lambda: on(hops - 2, reduce_and_give))
    on(hops - 1, reduce_block)
    on(hops, reduce_block)
    on(hops - 1, give_all)
    on(hops, give_all)

    def stats(p):
        drain(lstat.at[pl.ds(1, D * S - 1), p], st_send.at[p], st_recv.at[p]).wait_recv()
        for b in range(D):
            m = lstat[b * S, p, 0:1, :]
            for k in range(1, S):
                m = jnp.maximum(m, lstat[b * S + k, p, 0:1, :])
            total = jnp.zeros_like(m)
            for k in range(S):
                total = total + lstat[b * S + k, p, 1:2, :] * jnp.exp(lstat[b * S + k, p, 0:1, :] - m)
            zstat[z, b, 0, pl.ds(p, 1), :] = m
            zstat[z, b, 1, pl.ds(p, 1), :] = total
            zstat[z, b, 2, pl.ds(p, 1), :] = lstat[b * S, p, 2:3, :]

    if O > 8:
        lax.fori_loop(0, O, lambda p, carry: (stats(p), carry)[1], 0)
    else:
        for p in range(O):
            stats(p)

    def column(o):
        return pltpu.make_async_remote_copy(
            src_ref=zstat.at[z], dst_ref=zstat.at[z], send_sem=z_send, recv_sem=z_recv,
            device_id=dev(lax.rem(z + o, O), d, s), device_id_type=MESH)

    for o in range(1, O):
        column(o).start()

    def dom_wait(p, carry):
        @pl.when(used(p))
        def _():
            for od in range(1, D):
                across(od, p).wait_recv()
                keep_copy(lax.rem(d + D - od, D), p).start()
        return carry

    lax.fori_loop(0, O, dom_wait, 0)

    @pl.when(owner == d)
    def _():
        drain(erecv.at[pl.ds(1, S - 1)], e_send, e_recv).wait_recv()

    @pl.when(owner != d)
    def _():
        drain(erecv, e_send, e_recv).wait_recv()

    drain(zstat.at[pl.ds(1, O - 1)], z_send, z_recv).wait_recv()
    for b in range(D):
        m_all, t_all, name = zstat[:, b, 0], zstat[:, b, 1], zstat[:, b, 2]
        for j in range(O):
            mine = name == j
            m = jnp.max(jnp.max(jnp.where(mine, m_all, floor_value), axis=0), axis=0, keepdims=True)
            total = jnp.where(mine, t_all * jnp.exp(jnp.where(mine, m_all - m, 0.0)), 0.0)
            total = jnp.sum(jnp.sum(total, axis=0), axis=0, keepdims=True)
            logn[b, j] = m + jnp.log(total)

    pick = logn[d, 0]
    for j in range(1, O):
        pick = jnp.where(z == j, logn[d, j], pick)
    home_ref[...] = pick

    def posterior(b, q, p):
        k = d * per + q
        name = lstat[b * S + k, p, 2:3, :]
        whole = jnp.zeros_like(name)
        for j in range(max(p - skip, 0), min(p + skip, O - 1) + 1):
            whole = jnp.where(name == j, logn[b, j], whole)
        scale = jnp.exp(lstat[b * S + k, p, 0:1, :] - whole)
        return (erecv[b * per + q, p].astype(jnp.float32) * scale).astype(jnp.bfloat16)

    for q in range(per):
        for b in range(D):
            for p in range(0, O, 2):
                both = [posterior(b, q, i) for i in range(p, min(p + 2, O))]
                at = slice((b * O + p) * img_rows, (b * O + p + len(both)) * img_rows)
                prob_ref[q * lanes:(q + 1) * lanes, at] = jnp.concatenate(both, axis=1)

    def sent(p, carry):
        @pl.when(used(p))
        def _():
            for od in range(1, D):
                across(od, p).wait_send()
            drain(recvp.at[p], rs_send.at[p], rs_recv.at[p]).wait_send()
        drain(lstat.at[pl.ds(1, D * S - 1), p], st_send.at[p], st_recv.at[p]).wait_send()

        for side, edge, before in ((0, O - 1, O - 2), (1, 0, 1)):
            beyond = p <= z if side == 0 else p >= z
            went = (z != edge) & beyond
            if skip:
                near_edge = (z == before) & ((p >= O - 1 - room) if side == 0 else (p <= room))
                went = went & ((z != before) | near_edge)

            @pl.when(went)
            def _():
                sem = up_sem if side == 0 else dn_sem
                drain(images.at[d, p], sem.at[p], img_sem.at[p, 0]).wait_send()
        return carry

    lax.fori_loop(0, O, sent, 0)
    @pl.when(owner == d)
    def _():
        drain(erecv.at[pl.ds(1, S - 1)], e_send, e_recv).wait_send()

    @pl.when(owner != d)
    def _():
        drain(erecv, e_send, e_recv).wait_send()

    drain(zstat.at[pl.ds(1, O - 1)], z_send, z_recv).wait_send()
    pltpu.make_async_copy(keep_ref, keep_ref, out_sem).wait()
    if skip:
        for side, edge in ((0, O - 1), (1, 0)):
            @pl.when(z == edge)
            def _():
                kept_copy(side).wait_send()


def product(prob_ref, home_ref, images, out_ref, logn_ref, total, out_sem):
    halves, width, wide = 2, images.shape[2], 512

    def put(c, n):
        cols = pl.ds(n * wide, wide)
        return pltpu.make_async_copy(
            total.at[c, :, cols], out_ref.at[:, c, cols], out_sem.at[c, n])

    logn_ref[...] = home_ref[...]
    for c in range(halves):
        for n in range(width // wide):
            cols = slice(n * wide, (n + 1) * wide)
            total[c, :, cols] = jnp.dot(
                prob_ref[...], images[c, :, cols], preferred_element_type=jnp.float32)
            put(c, n).start()
    for c in range(halves):
        for n in range(width // wide):
            put(c, n).wait()


def grant(shapes):
    total = 6 * 1024 * 1024
    for item in shapes:
        if getattr(item, "memory_space", None) == pltpu.VMEM:
            size = jnp.dtype(item.dtype).itemsize
            *lead, tall, wide = item.shape
            tall, wide = -(-tall // 8) * 8, -(-wide // 128) * 128
            total += math.prod(lead) * tall * wide * size
    return total


def shards(references, images, noise_var, shell_of, kept_blocks):
    O, D, S = (lax.axis_size(a) for a in ("orient", "dom", "shell"))
    rows = references.shape[0]
    img_rows = images.shape[0]
    local = references.shape[2]
    flat = 2 * local
    lanes = rows // S
    own = rows // D
    columns = O * img_rows
    vmem = pl.BlockSpec(memory_space=pltpu.VMEM)
    sem = pltpu.SemaphoreType.DMA
    f32, bf16 = jnp.float32, jnp.bfloat16
    most = kept_blocks.shape[2]
    skip = max(O - most, 0)
    room = O - 1 - skip
    first = [
        pltpu.VMEM((D, O, 2, img_rows, local), bf16),
        pltpu.VMEM((2, room if skip else 1, 2, img_rows, local), bf16),
        pltpu.VMEM((most, 1, local), f32),
        pltpu.VMEM((2, most, 1, local), f32),
        pltpu.VMEM((2, O, 1, local), f32),
        pltpu.VMEM((O, S, img_rows, lanes), f32),
        pltpu.VMEM((O, S - 1, img_rows, lanes), f32),
        pltpu.VMEM((2, img_rows // 2, rows), f32),
        pltpu.VMEM((rows, flat), bf16),
        pltpu.VMEM((rows, 2, local), bf16),
        pltpu.VMEM((img_rows, 2, local), bf16),
        pltpu.VMEM((O, lanes, img_rows), bf16),
        pltpu.VMEM((S, O, lanes, img_rows), bf16),
        pltpu.VMEM((D * S, O, 4, img_rows), f32),
        pltpu.VMEM((O, D, 3, O, img_rows), f32),
        pltpu.VMEM((D, O, 1, img_rows), f32),
        pltpu.VMEM((1, local), f32),
        pltpu.VMEM((S, 1, lanes), f32),
        pltpu.VMEM((1, local), jnp.int32),
        pltpu.SMEM((most,), jnp.int32),
        pltpu.SMEM(noise_var.shape, f32),
        pltpu.SMEM((O,), jnp.int32),
        sem((O,)), sem((O,)), sem((O, 8)),
        sem((D - 1, O)), sem((D - 1, O)),
        sem((O,)), sem((O,)),
        sem((O,)), sem((O,)),
        sem, sem,
        sem, sem, sem((2,)), sem((2,)),
        sem, sem((5,)),
    ]
    probs, home, kept_images = pl.pallas_call(
        functools.partial(kernel, (O, D, S)),
        name="expectation",
        out_shape=(
            jax.ShapeDtypeStruct((own, D * columns), bf16),
            jax.ShapeDtypeStruct((1, img_rows), f32),
            jax.ShapeDtypeStruct((2, D, O, img_rows, local), bf16),
        ),
        in_specs=[pl.BlockSpec(memory_space=pltpu.HBM)] * 5,
        out_specs=(vmem, vmem, pl.BlockSpec(memory_space=pl.ANY)),
        scratch_shapes=first,
        compiler_params=pltpu.CompilerParams(collective_id=0, has_side_effects=True, vmem_limit_bytes=grant(first)),
    )(
        pltpu.with_memory_space_constraint(kept_blocks.reshape(-1), pltpu.HBM),
        pltpu.with_memory_space_constraint(noise_var, pltpu.HBM),
        pltpu.with_memory_space_constraint(shell_of.reshape(1,-1), pltpu.HBM),
        pltpu.with_memory_space_constraint(references, pltpu.HBM),
        pltpu.with_memory_space_constraint(images, pltpu.HBM),
    )
    depth = D * columns
    second = [
        pltpu.VMEM((2, own, local), f32),
        sem((2, local // 512)),
    ]
    weighted, log_norm = pl.pallas_call(
        product,
        name="product",
        out_shape=(
            jax.ShapeDtypeStruct((own, 2, local), f32),
            jax.ShapeDtypeStruct((1, img_rows), f32),
        ),
        in_specs=[vmem, vmem, vmem],
        out_specs=(pl.BlockSpec(memory_space=pl.ANY), vmem),
        scratch_shapes=second,
        compiler_params=pltpu.CompilerParams(vmem_limit_bytes=grant(second)),
    )(probs, home, kept_images.reshape(2, depth, local))
    return weighted, log_norm.reshape(img_rows)


def solution(mesh):
    placed = (
        P("orient", None, "shell"),
        P(("orient", "dom"), None, "shell"),
        P(),
        P("shell"),
        P("orient", "dom", None),
    )
    return jax.shard_map(
        shards,
        mesh=mesh,
        in_specs=placed,
        out_specs=(P(("orient", "dom"), None, "shell"), P(("orient", "dom"))),
        check_vma=False,
    )
```

time: 40.7 us -> 37.3 us (0.916)
  Pallas kernels: 39.8 us -> 36.3 us
    pallas_call x1, Pallas kernels: 37.3 us -> 33.8 us  [shards(): pl.pallas_call(functools.partial(kernel, (O, D, S)), name='expectation',...]
where the time goes in v2:
time: 37.3 us; the launch traced here: 37.1 us
  Pallas kernels  36.3 us (97%)
  between operations  0.8 us (2%)
    pallas_call x1, Pallas kernels, shards(): pl.pallas_call(functools.partial(kernel, (O, D, S)), name='expectation',...  33.8 us
    pallas_call x1, Pallas kernels, shards(): pl.pallas_call(product, name='product', out_shape=(jax.ShapeDtypeStruct((...  2.58 us

profile of v2, /device:TPU:0, one launch (start us, length us, event | category | flops | bytes accessed | tf_op | source)
XLA Modules:
  0.0 37.1 jit_solution(15945556450906313834)
XLA Ops:
  0.6 33.8 %expectation.1 = (bf16[256,512]{1,0:T(8,128)(2,1)S(1)}, f32[1,64]{1,0:T(1,128)S(1)}, bf16[2,2,4,64,1024]{4,3,2,1,0:T(8,128)(2,1)S(1)}) custom-call(s32[3]{0:T(128)} %bitcast.6, f32[64]{0:T(128)} %noise_hbm.1, s32[1,1024]{1,0:T(1,128)} %bitcast.5, bf16[512,2,1024]{2,1,0:T(2,128)(2,1)} %raw_ref.1, bf16[64,2,1024]{2,1,0:T(2,128)(2,1)} %whole_ref.1), custom_call_target="tpu_custom_call" | custom-call | tf_op jit(solution)/shard_map/expectation/pallas_call | solution.py:604
  34.4 2.6 %product.1 = (f32[256,2,1024]{2,1,0:T(2,128)}, f32[1,64]{1,0:T(1,128)}) custom-call(bf16[256,512]{1,0:T(8,128)(2,1)S(1)} %get-tuple-element.7.prob_ref, f32[1,64]{1,0:T(1,128)S(1)} %get-tuple-element.8.home_ref, bf16[2,512,1024]{2,1,0:T(8,128)(2,1)S(1)} %bitcast.4), custom_call_target="tpu_custom_call" | custom-call | tf_op jit(solution)/shard_map/product/pallas_call | solution.py:628

commit v3 on v2

--- a/solution.py
+++ b/solution.py
@@ -10,15 +10,27 @@
 
 floor_value = -1e30
 MESH = pl.DeviceIdType.MESH
-ahead = 2
+
+
+def farthest(O, most):
+    skip = max(O - most, 0)
+    room = O - 1 - skip
+    hops = max(O - 2, room)
+    found = {}
+    for y in range(O):
+        for p in (y - hops, y + hops):
+            off = skip and ((y == O - 1 and p < skip) or (y == 0 and p > room))
+            if 0 <= p < O and not off:
+                found[y] = p
+    return found
 
 
 def kernel(
     sizes, kept_hbm, noise_hbm, shell_hbm, raw_ref, whole_ref, prob_ref, home_ref, keep_ref,
-    images, slots, kout, kin, shift, part, recvp, held, refs_ref, stage, img_stage,
-    ebuf, erecv, lstat, zstat, logn, w_s, rn_s, shell_ref, kept_ref, noise_ref, ids,
+    images, slots, kout, kin, shift, part, recvp, held, full_held, refs_ref, stage, img_stage,
+    ebuf, erecv, lstat, zstat, fstat, logn, w_s, rn_s, shell_ref, kept_ref, noise_ref, ids,
     up_sem, dn_sem, img_sem, dom_send, dom_recv, rs_send, rs_recv, st_send, st_recv,
-    e_send, e_recv, z_send, z_recv, k_send, k_recv, out_sem, in_sem,
+    e_send, e_recv, z_send, z_recv, k_send, k_recv, f_send, f_recv, out_sem, in_sem,
 ):
     O, D, S = sizes
     z, d, s = lax.axis_index("orient"), lax.axis_index("dom"), lax.axis_index("shell")
@@ -44,8 +56,8 @@
             (whole_ref, img_stage), (raw_ref, stage), (kept_hbm, kept_ref),
             (noise_hbm, noise_ref), (shell_hbm, shell_ref)))
     ]
-    for copy in inputs:
-        copy.start()
+    inputs[0].start()
+    inputs[2].start()
     barrier = pltpu.get_barrier_semaphore()
     for ok, to in ((z < O - 1, z + 1), (z > 0, z + O - 1)):
         @pl.when(ok)
@@ -62,6 +74,9 @@
                     device_id_type=MESH,
                 )
 
+    for i in (1, 3, 4):
+        inputs[i].start()
+
     def used(p):
         if not skip:
             return p >= 0
@@ -100,9 +115,12 @@
         c, at = piece(n)
         first = step(side, z, k)
         v = images[d, first, c, at].astype(jnp.float32)
-        for m in range(1, skip + 1):
+
+        def take(m, v):
             other = images[d, step(side, first, m), c, at].astype(jnp.float32)
-            v = jnp.where(shift[side, k + m] == m, other, v)
+            return jnp.where(shift[side, k + m] == m, other, v)
+
+        v = lax.fori_loop(1, skip + 1, take, v, unroll=skip < 3)
         slots[side, k, c, at] = v.astype(jnp.bfloat16)
 
     def relay(side, t, n):
@@ -169,15 +187,41 @@
             def _():
                 give(p, to).start()
 
-    def publish(p, m, total, name, e):
-        mine = d * S + s
-        lstat[mine, p, 0:1, :] = m
-        lstat[mine, p, 1:2, :] = total
-        lstat[mine, p, 2:3, :] = name
-        lstat[mine, p, 3:4, :] = jnp.zeros_like(m)
+    last_of = farthest(O, most)
+    lasts = list(last_of)
+    rank = sum(jnp.where(z == y, i, 0) for i, y in enumerate(lasts))
+    member = functools.reduce(jnp.logical_or, [z == y for y in lasts])
+    last_here = sum(jnp.where(z == y, p, 0) for y, p in last_of.items())
+    last_here = jnp.where(member, last_here, -1)
+
+    def everywhere():
+        mine = (rank * D + d) * S + s
+        for i in range(O):
+            y = jnp.where(z < O // 2, O - 1 - i, i)
+            for od, os in peers[::-1] + [(0, 0)]:
+                copy = pltpu.make_async_remote_copy(
+                    src_ref=fstat.at[mine], dst_ref=fstat.at[mine], send_sem=f_send,
+                    recv_sem=f_recv,
+                    device_id=dev(y, lax.rem(d + od, D), lax.rem(s + os, S)),
+                    device_id_type=MESH)
+                if od or os:
+                    copy.start()
+                else:
+                    pl.when(y != z)(copy.start)
+
+    def publish(p, m, total, name, e, last=False):
+        mine = (rank * D + d) * S + s if last else d * S + s
+        ref = fstat.at[mine] if last else lstat.at[mine, p]
+        ref[0:1, :] = m
+        ref[1:2, :] = total
+        ref[2:3, :] = name
+        ref[3:4, :] = jnp.zeros_like(m)
+        if last:
+            everywhere()
+        else:
+            for od, os in peers:
+                spread(p, od, os).start()
         ebuf[p] = e
-        for od, os in peers:
-            spread(p, od, os).start()
 
         @pl.when(owner == d)
         def _():
@@ -214,7 +258,7 @@
         at = pl.ds(h * hr, hr)
         for k in range(S):
             part[p, k, at] = full[:, k * lanes:(k + 1) * lanes] - rn_s[k]
-        for o in range(1, S):
+        for o in sorted(range(1, S), key=lambda o: o % 2 == 0):
             scatter(p, h, o).start()
 
     def whole_block(p, side):
@@ -223,7 +267,7 @@
         for h in range(2):
             finish(full[h * hr:(h + 1) * hr], p, h)
 
-    def reduce_block(p, side):
+    def reduce_block(p, side, last=False):
         drain(recvp.at[p], rs_send.at[p], rs_recv.at[p]).wait_recv()
         v = part[p, s]
         for o in range(S - 1):
@@ -237,18 +281,7 @@
         m = jnp.max(v, axis=0, keepdims=True)
         e = jnp.where(keep, jnp.exp(v - m), 0.0)
         total = jnp.sum(e, axis=0, keepdims=True)
-        publish(p, m, total, want[:1].astype(jnp.float32), e.astype(jnp.bfloat16))
-
-    inputs[0].wait()
-    x = img_stage[...]
-    for c in range(2):
-        images[d, z, c] = x[:, c, :]
-    inputs[2].wait()
-    inputs[1].wait()
-    for n in range(ahead):
-        spread_rows(n)
-    near = jnp.where(z < O - 1, 1, 0) + jnp.where(z > 0, 1, 0)
-    pl.semaphore_wait(barrier, near + D * S - 1)
+        publish(p, m, total, want[:1].astype(jnp.float32), e.astype(jnp.bfloat16), last)
 
     def kept_copy(side):
         to = lax.rem(z + O - 1, O) if side == 0 else lax.rem(z + 1, O)
@@ -256,21 +289,37 @@
             src_ref=kout, dst_ref=kin.at[side], send_sem=k_send.at[side],
             recv_sem=k_recv.at[side], device_id=dev(to, d, s), device_id_type=MESH)
 
+    def own_rows(h):
+        at = slice(h * hr, (h + 1) * hr)
+        x = img_stage[at]
+        for c in range(2):
+            images[d, z, c, at] = x[:, c, :]
+
+    between = (z > 0) & (z < O - 1)
+    tip = jnp.logical_not(between)
+    inputs[2].wait()
     if skip:
-        @pl.when((z == 0) | (z == O - 1))
+        @pl.when(tip)
         def _():
             for k in range(most):
-                kout[k] = jnp.full((1, half), kept_ref[k], jnp.int32).astype(jnp.float32)
-        for side, edge in ((0, O - 1), (1, 0)):
-            @pl.when(z == edge)
+                kout[k] = jnp.full((1, 128), kept_ref[k], jnp.int32).astype(jnp.float32)
+    inputs[0].wait()
+    own_rows(0)
+    near = jnp.where(z < O - 1, 1, 0) + jnp.where(z > 0, 1, 0)
+    pl.semaphore_wait(barrier, near + D * S - 1)
+    if skip:
+        for side, last in ((0, O - 1), (1, 0)):
+            @pl.when(z == last)
             def _():
                 kept_copy(side).start()
-
-    for n in range(chunks):
-        for side in range(2):
-            relay(side, 0, n)
-
+    for h in range(2):
+        if h:
+            own_rows(h)
+        for n in range(4 * h, 4 * h + 4):
+            for side in range(2):
+                relay(side, 0, n)
     landed(z, 0)
+    inputs[1].wait()
 
     def candidate(side, c):
         return O - 2 - c if side == 0 else 1 + c
@@ -310,10 +359,11 @@
             @pl.when(z == before)
             def _():
                 kept_copy(side).wait_recv()
-                gone = jnp.zeros((1, half), jnp.float32)
+                gone = jnp.zeros((1, 128), jnp.float32)
                 for c in range(O - 1):
-                    shift[side, c] = jnp.minimum(gone, skip)
-                    need = jnp.zeros((1, half), jnp.float32)
+                    moved = jnp.minimum(gone, skip)
+                    shift[side, c] = jnp.concatenate([moved] * (half // 128), axis=1)
+                    need = jnp.zeros((1, 128), jnp.float32)
                     for k in range(most):
                         need = jnp.where(kin[side, k] == candidate(side, c), 1.0, need)
                     gone = gone + 1.0 - need
@@ -327,9 +377,6 @@
             noise = jnp.where(shell == i, noise_ref[i], noise)
         w_s[...] = 1.0 / noise
 
-    between = (z > 0) & (z < O - 1)
-    edge = jnp.logical_not(between)
-
     def on_side(side, t, act):
         @pl.when(has(side, t))
         def _():
@@ -344,11 +391,10 @@
             serve(t, n)
             for job in jobs.get(n, ()):
                 job()
-        on(t, landed)
-
-    @pl.when(edge)
-    def _():
-        for n in range(ahead, pieces):
+
+    @pl.when(tip)
+    def _():
+        for n in range(pieces):
             spread_rows(n)
         weights()
         for c in range(S):
@@ -356,29 +402,31 @@
         whole_block(z, 0)
         run(1, {})
         on(1, whole_block)
+        on(1, landed)
         reduce_and_give(z, 0)
 
     @pl.when(between)
     def _():
-        for n in range(ahead, ahead + 2):
+        for n in range(3):
             spread_rows(n)
         shifts()
-        rest = [functools.partial(spread_rows, n) for n in range(ahead + 2, pieces)]
-        rest += [weights] + [functools.partial(norm_rows, c) for c in range(S)]
-        jobs = {n: [rest[n]] for n in range(4)}
-        jobs[4] = rest[4:6]
-        jobs[5] = rest[6:]
-        jobs[6] = [lambda: whole_block(z, 0)]
+        jobs = {n: [functools.partial(spread_rows, n + 3)] for n in range(pieces - 3)}
+        norms = [functools.partial(norm_rows, c) for c in range(S)]
+        jobs[5] = [weights] + norms[:S // 2]
+        jobs[6] = norms[S // 2:]
         run(1, jobs)
+        on(1, landed)
 
     def middle(t, carry):
-        pl.when(edge & (t > 2))(lambda: on(t - 1, whole_block))
+        pl.when(tip & (t > 2))(lambda: on(t - 1, whole_block))
+        pl.when(between & (t == 2))(lambda: whole_block(z, 0))
         run(t, {
             0: [lambda: pl.when(between)(lambda: on_side(0, t - 1, whole_block))],
             2: [lambda: pl.when(between)(lambda: on_side(1, t - 1, whole_block))],
             4: [lambda: pl.when((t > 2) | between)(lambda: on_side(0, t - 2, reduce_and_give))],
             5: [lambda: pl.when(t > 2)(lambda: on_side(1, t - 2, reduce_and_give))],
         })
+        on(t, landed)
         return carry
 
     lax.fori_loop(2, hops, middle, 0)
@@ -395,32 +443,76 @@
         finish(held[side] + cross(p, 1, high), p, 1)
 
     if hops > 2:
-        pl.when(edge)(lambda: on(hops - 1, whole_block))
-    run(hops, {
-        0: [lambda: pl.when(between)(lambda: on_side(0, hops - 1, whole_block))],
-        2: [lambda: pl.when(between)(lambda: on_side(1, hops - 1, whole_block))],
-        3: [lambda: on(hops, first_half)],
-        5: [lambda: on(hops, third_quarter)],
-        7: [lambda: on(hops, last_quarter)],
-    })
+        pl.when(tip)(lambda: on(hops - 1, whole_block))
+    def first_product(p, side):
+        full_held[...] = cross(p, 0, slice(0, img_rows))
+
+    def second_product(p, side):
+        full = full_held[...] + cross(p, 1, slice(0, img_rows))
+        for h in range(2):
+            finish(full[h * hr:(h + 1) * hr], p, h)
+
+    def mid(act):
+        return lambda: pl.when(between)(act)
+
+    jobs = {
+        1: [mid(lambda: on_side(0, hops - 1, first_product))],
+        2: [mid(lambda: on_side(0, hops - 1, second_product))],
+        3: [mid(lambda: on_side(1, hops - 1, first_product)),
+            lambda: pl.when(tip)(lambda: on(hops, first_half))],
+        4: [mid(lambda: on_side(1, hops - 1, second_product))],
+        5: [lambda: pl.when(tip)(lambda: on(hops, third_quarter))],
+        6: [lambda: pl.when(tip)(lambda: on(hops - 1, reduce_block))],
+    }
+    if hops == 2:
+        jobs[0] = [mid(lambda: whole_block(z, 0))]
+    run(hops, jobs)
+
+    @pl.when(between)
+    def _():
+        on(hops, first_half)
+        on(hops, third_quarter)
+
+    on(hops, last_quarter)
+
+    @pl.when(tip)
+    def _():
+        on(hops - 1, give_all)
+
     pl.when(between if hops == 2 else z >= 0)(lambda: on(hops - 2, reduce_and_give))
-    on(hops - 1, reduce_block)
-    on(hops, reduce_block)
-    on(hops - 1, give_all)
+
+    @pl.when(between)
+    def _():
+        on(hops - 1, reduce_and_give)
+
+    on(hops, functools.partial(reduce_block, last=True))
+    on(hops, landed)
     on(hops, give_all)
 
+    def combine(rows, at):
+        m = rows[0][0:1, :]
+        for row in rows[1:]:
+            m = jnp.maximum(m, row[0:1, :])
+        total = jnp.zeros_like(m)
+        for row in rows:
+            total = total + row[1:2, :] * jnp.exp(row[0:1, :] - m)
+        y, b, p = at
+        zstat[y, b, 0, pl.ds(p, 1), :] = m
+        zstat[y, b, 1, pl.ds(p, 1), :] = total
+        zstat[y, b, 2, pl.ds(p, 1), :] = rows[0][2:3, :]
+
     def stats(p):
-        drain(lstat.at[pl.ds(1, D * S - 1), p], st_send.at[p], st_recv.at[p]).wait_recv()
-        for b in range(D):
-            m = lstat[b * S, p, 0:1, :]
-            for k in range(1, S):
-                m = jnp.maximum(m, lstat[b * S + k, p, 0:1, :])
-            total = jnp.zeros_like(m)
-            for k in range(S):
-                total = total + lstat[b * S + k, p, 1:2, :] * jnp.exp(lstat[b * S + k, p, 0:1, :] - m)
-            zstat[z, b, 0, pl.ds(p, 1), :] = m
-            zstat[z, b, 1, pl.ds(p, 1), :] = total
-            zstat[z, b, 2, pl.ds(p, 1), :] = lstat[b * S, p, 2:3, :]
+        @pl.when(last_here != p)
+        def _():
+            drain(lstat.at[pl.ds(1, D * S - 1), p], st_send.at[p], st_recv.at[p]).wait_recv()
+            for b in range(D):
+                combine([lstat[b * S + k, p] for k in range(S)], (z, b, p))
+
+        @pl.when(last_here == p)
+        def _():
+            for b in range(D):
+                for row, value in enumerate((floor_value, 0.0, -2.0)):
+                    zstat[z, b, row, pl.ds(p, 1), :] = jnp.full((1, img_rows), value, jnp.float32)
 
     if O > 8:
         lax.fori_loop(0, O, lambda p, carry: (stats(p), carry)[1], 0)
@@ -455,14 +547,36 @@
         drain(erecv, e_send, e_recv).wait_recv()
 
     drain(zstat.at[pl.ds(1, O - 1)], z_send, z_recv).wait_recv()
+    drain(zstat.at[pl.ds(1, O - 1)], z_send, z_recv).wait_send()
+
+    @pl.when(member)
+    def _():
+        drain(fstat.at[pl.ds(1, len(lasts) * D * S - 1)], f_send, f_recv).wait_recv()
+        for k in range(D * S):
+            lstat[k, last_here] = fstat[rank * D * S + k]
+
+    if len(lasts) < O:
+        @pl.when(jnp.logical_not(member))
+        def _():
+            drain(fstat, f_send, f_recv).wait_recv()
+
+    for i, (y, p) in enumerate(last_of.items()):
+        for b in range(D):
+            combine([fstat[(i * D + b) * S + k] for k in range(S)], (y, b, p))
     for b in range(D):
-        m_all, t_all, name = zstat[:, b, 0], zstat[:, b, 1], zstat[:, b, 2]
-        for j in range(O):
-            mine = name == j
+        def norm(j, carry, b=b):
+            m_all, t_all, mine = zstat[:, b, 0], zstat[:, b, 1], zstat[:, b, 2] == jnp.asarray(j, jnp.float32)
             m = jnp.max(jnp.max(jnp.where(mine, m_all, floor_value), axis=0), axis=0, keepdims=True)
             total = jnp.where(mine, t_all * jnp.exp(jnp.where(mine, m_all - m, 0.0)), 0.0)
             total = jnp.sum(jnp.sum(total, axis=0), axis=0, keepdims=True)
             logn[b, j] = m + jnp.log(total)
+            return carry
+
+        if O > 8:
+            lax.fori_loop(0, O, norm, 0)
+        else:
+            for j in range(O):
+                norm(j, 0)
 
     pick = logn[d, 0]
     for j in range(1, O):
@@ -491,7 +605,10 @@
             for od in range(1, D):
                 across(od, p).wait_send()
             drain(recvp.at[p], rs_send.at[p], rs_recv.at[p]).wait_send()
-        drain(lstat.at[pl.ds(1, D * S - 1), p], st_send.at[p], st_recv.at[p]).wait_send()
+
+        @pl.when(last_here != p)
+        def _():
+            drain(lstat.at[pl.ds(1, D * S - 1), p], st_send.at[p], st_recv.at[p]).wait_send()
 
         for side, edge, before in ((0, O - 1, O - 2), (1, 0, 1)):
             beyond = p <= z if side == 0 else p >= z
@@ -515,7 +632,15 @@
     def _():
         drain(erecv, e_send, e_recv).wait_send()
 
-    drain(zstat.at[pl.ds(1, O - 1)], z_send, z_recv).wait_send()
+    @pl.when(member)
+    def _():
+        if len(lasts) == O:
+            drain(fstat.at[pl.ds(1, O * D * S - 1)], f_send, f_recv).wait_send()
+        else:
+            for y in range(O - 1):
+                drain(lstat.at[:, 0], f_send, f_recv).wait_send()
+            drain(lstat.at[pl.ds(1, D * S - 1), 0], f_send, f_recv).wait_send()
+
     pltpu.make_async_copy(keep_ref, keep_ref, out_sem).wait()
     if skip:
         for side, edge in ((0, O - 1), (1, 0)):
@@ -525,7 +650,7 @@
 
 
 def product(prob_ref, home_ref, images, out_ref, logn_ref, total, out_sem):
-    halves, width, wide = 2, images.shape[2], 512
+    halves, width, wide = 2, images.shape[2], 1024
 
     def put(c, n):
         cols = pl.ds(n * wide, wide)
@@ -573,12 +698,13 @@
     first = [
         pltpu.VMEM((D, O, 2, img_rows, local), bf16),
         pltpu.VMEM((2, room if skip else 1, 2, img_rows, local), bf16),
-        pltpu.VMEM((most, 1, local), f32),
-        pltpu.VMEM((2, most, 1, local), f32),
+        pltpu.VMEM((most, 1, 128), f32),
+        pltpu.VMEM((2, most, 1, 128), f32),
         pltpu.VMEM((2, O, 1, local), f32),
         pltpu.VMEM((O, S, img_rows, lanes), f32),
         pltpu.VMEM((O, S - 1, img_rows, lanes), f32),
         pltpu.VMEM((2, img_rows // 2, rows), f32),
+        pltpu.VMEM((img_rows, rows), f32),
         pltpu.VMEM((rows, flat), bf16),
         pltpu.VMEM((rows, 2, local), bf16),
         pltpu.VMEM((img_rows, 2, local), bf16),
@@ -586,6 +712,7 @@
         pltpu.VMEM((S, O, lanes, img_rows), bf16),
         pltpu.VMEM((D * S, O, 4, img_rows), f32),
         pltpu.VMEM((O, D, 3, O, img_rows), f32),
+        pltpu.VMEM((len(farthest(O, most)) * D * S, 4, img_rows), f32),
         pltpu.VMEM((D, O, 1, img_rows), f32),
         pltpu.VMEM((1, local), f32),
         pltpu.VMEM((S, 1, lanes), f32),
@@ -599,7 +726,7 @@
         sem((O,)), sem((O,)),
         sem, sem,
         sem, sem, sem((2,)), sem((2,)),
-        sem, sem((5,)),
+        sem, sem, sem, sem((5,)),
     ]
     probs, home, kept_images = pl.pallas_call(
         functools.partial(kernel, (O, D, S)),
@@ -623,7 +750,7 @@
     depth = D * columns
     second = [
         pltpu.VMEM((2, own, local), f32),
-        sem((2, local // 512)),
+        sem((2, local // 1024)),
     ]
     weighted, log_norm = pl.pallas_call(
         product,

time: 37.3 us -> 34.6 us (0.928)
  Pallas kernels: 36.3 us -> 33.7 us
    pallas_call x1, Pallas kernels: 33.8 us -> 31.3 us  [shards(): pl.pallas_call(functools.partial(kernel, (O, D, S)), name='expectation',...]
where the time goes in v3:
time: 34.6 us; the launch traced here: 34.5 us
  Pallas kernels  33.7 us (97%)
  between operations  0.8 us (2%)
    pallas_call x1, Pallas kernels, shards(): pl.pallas_call(functools.partial(kernel, (O, D, S)), name='expectation',...  31.3 us
    pallas_call x1, Pallas kernels, shards(): pl.pallas_call(product, name='product', out_shape=(jax.ShapeDtypeStruct((...  2.4 us

profile of v3, /device:TPU:0, one launch (start us, length us, event | category | flops | bytes accessed | tf_op | source)
XLA Modules:
  0.0 34.5 jit_solution(4890680648266653680)
XLA Ops:
  0.6 31.3 %expectation.1 = (bf16[256,512]{1,0:T(8,128)(2,1)S(1)}, f32[1,64]{1,0:T(1,128)S(1)}, bf16[2,2,4,64,1024]{4,3,2,1,0:T(8,128)(2,1)S(1)}) custom-call(s32[3]{0:T(128)} %bitcast.6, f32[64]{0:T(128)} %noise_hbm.1, s32[1,1024]{1,0:T(1,128)} %bitcast.5, bf16[512,2,1024]{2,1,0:T(2,128)(2,1)} %raw_ref.1, bf16[64,2,1024]{2,1,0:T(2,128)(2,1)} %whole_ref.1), custom_call_target="tpu_custom_call" | custom-call | tf_op jit(solution)/shard_map/expectation/pallas_call | solution.py:731
  31.9 2.4 %product.1 = (f32[256,2,1024]{2,1,0:T(2,128)}, f32[1,64]{1,0:T(1,128)}) custom-call(bf16[256,512]{1,0:T(8,128)(2,1)S(1)} %get-tuple-element.7.prob_ref, f32[1,64]{1,0:T(1,128)S(1)} %get-tuple-element.8.home_ref, bf16[2,512,1024]{2,1,0:T(8,128)(2,1)S(1)} %bitcast.4), custom_call_target="tpu_custom_call" | custom-call | tf_op jit(solution)/shard_map/product/pallas_call | solution.py:755

commit v4 on v3

--- a/solution.py
+++ b/solution.py
@@ -105,8 +105,8 @@
         to = lax.rem(z + 1, O) if side == 0 else lax.rem(z + O - 1, O)
         send = up_sem if side == 0 else dn_sem
         return pltpu.make_async_remote_copy(
-            src_ref=src.at[c, at], dst_ref=images.at[d, p, c, at], send_sem=send.at[p],
-            recv_sem=img_sem.at[p, n], device_id=dev(to, d, s), device_id_type=MESH)
+            src_ref=src.at[c, at], dst_ref=images.at[d, p, c, at], send_sem=send,
+            recv_sem=img_sem.at[p - side, n], device_id=dev(to, d, s), device_id_type=MESH)
 
     def step(side, p, m):
         return p - m if side == 0 else p + m
@@ -150,7 +150,7 @@
     def across(od, p):
         return pltpu.make_async_remote_copy(
             src_ref=images.at[d, p], dst_ref=images.at[d, p],
-            send_sem=dom_send.at[od - 1, p], recv_sem=dom_recv.at[od - 1, p],
+            send_sem=dom_send.at[od - 1], recv_sem=dom_recv.at[od - 1, p],
             device_id=dev(z, lax.rem(d + od, D), s), device_id_type=MESH)
 
     def keep_copy(b, p):
@@ -165,7 +165,7 @@
         to = lax.rem(s + o, S)
         at = pl.ds(h * hr, hr)
         return pltpu.make_async_remote_copy(
-            src_ref=part.at[p, to, at], dst_ref=recvp.at[p, o - 1, at], send_sem=rs_send.at[p],
+            src_ref=part.at[p, to, at], dst_ref=recvp.at[p, o - 1, at], send_sem=rs_send,
             recv_sem=rs_recv.at[p], device_id=dev(z, d, to), device_id_type=MESH)
 
     peers = [(od, os) for od in range(D) for os in range(S) if od or os]
@@ -173,7 +173,7 @@
     def spread(p, od, os):
         return pltpu.make_async_remote_copy(
             src_ref=lstat.at[d * S + s, p], dst_ref=lstat.at[d * S + s, p],
-            send_sem=st_send.at[p], recv_sem=st_recv.at[p],
+            send_sem=st_send, recv_sem=st_recv.at[p],
             device_id=dev(z, lax.rem(d + od, D), lax.rem(s + os, S)), device_id_type=MESH)
 
     def give(p, to):
@@ -268,7 +268,7 @@
             finish(full[h * hr:(h + 1) * hr], p, h)
 
     def reduce_block(p, side, last=False):
-        drain(recvp.at[p], rs_send.at[p], rs_recv.at[p]).wait_recv()
+        drain(recvp.at[p], rs_send, rs_recv.at[p]).wait_recv()
         v = part[p, s]
         for o in range(S - 1):
             v = v + recvp[p, o]
@@ -286,7 +286,7 @@
     def kept_copy(side):
         to = lax.rem(z + O - 1, O) if side == 0 else lax.rem(z + 1, O)
         return pltpu.make_async_remote_copy(
-            src_ref=kout, dst_ref=kin.at[side], send_sem=k_send.at[side],
+            src_ref=kout, dst_ref=kin.at[side], send_sem=k_send,
             recv_sem=k_recv.at[side], device_id=dev(to, d, s), device_id_type=MESH)
 
     def own_rows(h):
@@ -504,7 +504,7 @@
     def stats(p):
         @pl.when(last_here != p)
         def _():
-            drain(lstat.at[pl.ds(1, D * S - 1), p], st_send.at[p], st_recv.at[p]).wait_recv()
+            drain(lstat.at[pl.ds(1, D * S - 1), p], st_send, st_recv.at[p]).wait_recv()
             for b in range(D):
                 combine([lstat[b * S + k, p] for k in range(S)], (z, b, p))
 
@@ -599,31 +599,33 @@
                 at = slice((b * O + p) * img_rows, (b * O + p + len(both)) * img_rows)
                 prob_ref[q * lanes:(q + 1) * lanes, at] = jnp.concatenate(both, axis=1)
 
-    def sent(p, carry):
-        @pl.when(used(p))
-        def _():
-            for od in range(1, D):
-                across(od, p).wait_send()
-            drain(recvp.at[p], rs_send.at[p], rs_recv.at[p]).wait_send()
-
-        @pl.when(last_here != p)
-        def _():
-            drain(lstat.at[pl.ds(1, D * S - 1), p], st_send.at[p], st_recv.at[p]).wait_send()
-
-        for side, edge, before in ((0, O - 1, O - 2), (1, 0, 1)):
-            beyond = p <= z if side == 0 else p >= z
-            went = (z != edge) & beyond
-            if skip:
-                near_edge = (z == before) & ((p >= O - 1 - room) if side == 0 else (p <= room))
-                went = went & ((z != before) | near_edge)
-
-            @pl.when(went)
-            def _():
-                sem = up_sem if side == 0 else dn_sem
-                drain(images.at[d, p], sem.at[p], img_sem.at[p, 0]).wait_send()
-        return carry
-
-    lax.fori_loop(0, O, sent, 0)
+    def sent(blocks):
+        for od in range(1, D):
+            drain(images.at[d, pl.ds(0, blocks)], dom_send.at[od - 1], dom_recv.at[0, 0]).wait_send()
+        drain(recvp.at[pl.ds(0, blocks)], rs_send, rs_recv.at[0]).wait_send()
+
+    pl.when(between)(lambda: sent(O))
+    pl.when(tip)(lambda: sent(room + 1))
+
+    def told(blocks):
+        every = lstat.at[pl.ds(1, D * S - 1), pl.ds(0, blocks)]
+        drain(every, st_send, st_recv.at[0]).wait_send()
+
+    pl.when(member)(lambda: told(O - 1))
+    if len(lasts) < O:
+        pl.when(jnp.logical_not(member))(lambda: told(O))
+
+    def passed(side, blocks):
+        sem = up_sem if side == 0 else dn_sem
+        drain(images.at[d, pl.ds(0, blocks)], sem, img_sem.at[0, 0]).wait_send()
+
+    for y in range(O):
+        for side in range(2):
+            ahead = y if side == 0 else O - 1 - y
+            if ahead < O - 1:
+                count = room if skip and ahead == O - 2 else ahead + 1
+                pl.when(z == y)(functools.partial(passed, side, count))
+
     @pl.when(owner == d)
     def _():
         drain(erecv.at[pl.ds(1, S - 1)], e_send, e_recv).wait_send()
@@ -720,12 +722,12 @@
         pltpu.SMEM((most,), jnp.int32),
         pltpu.SMEM(noise_var.shape, f32),
         pltpu.SMEM((O,), jnp.int32),
-        sem((O,)), sem((O,)), sem((O, 8)),
-        sem((D - 1, O)), sem((D - 1, O)),
-        sem((O,)), sem((O,)),
-        sem((O,)), sem((O,)),
+        sem, sem, sem((O - 1, 8)),
+        sem((D - 1,)), sem((D - 1, O)),
+        sem, sem((O,)),
+        sem, sem((O,)),
         sem, sem,
-        sem, sem, sem((2,)), sem((2,)),
+        sem, sem, sem, sem((2,)),
         sem, sem, sem, sem((5,)),
     ]
     probs, home, kept_images = pl.pallas_call(

time: 34.6 us -> 34.3 us (level)
  Pallas kernels: 33.7 us -> 33.3 us
where the time goes in v4:
time: 34.3 us; the launch traced here: 34.1 us
  Pallas kernels  33.3 us (97%)
  between operations  0.8 us (2%)
    pallas_call x1, Pallas kernels, shards(): pl.pallas_call(functools.partial(kernel, (O, D, S)), name='expectation',...  30.9 us
    pallas_call x1, Pallas kernels, shards(): pl.pallas_call(product, name='product', out_shape=(jax.ShapeDtypeStruct((...  2.4 us

profile of v4, /device:TPU:0, one launch (start us, length us, event | category | flops | bytes accessed | tf_op | source)
XLA Modules:
  0.0 34.1 jit_solution(5237526085528906963)
XLA Ops:
  0.6 30.9 %expectation.1 = (bf16[256,512]{1,0:T(8,128)(2,1)S(1)}, f32[1,64]{1,0:T(1,128)S(1)}, bf16[2,2,4,64,1024]{4,3,2,1,0:T(8,128)(2,1)S(1)}) custom-call(s32[3]{0:T(128)} %bitcast.6, f32[64]{0:T(128)} %noise_hbm.1, s32[1,1024]{1,0:T(1,128)} %bitcast.5, bf16[512,2,1024]{2,1,0:T(2,128)(2,1)} %raw_ref.1, bf16[64,2,1024]{2,1,0:T(2,128)(2,1)} %whole_ref.1), custom_call_target="tpu_custom_call" | custom-call | tf_op jit(solution)/shard_map/expectation/pallas_call | solution.py:733
  31.6 2.4 %product.1 = (f32[256,2,1024]{2,1,0:T(2,128)}, f32[1,64]{1,0:T(1,128)}) custom-call(bf16[256,512]{1,0:T(8,128)(2,1)S(1)} %get-tuple-element.7.prob_ref, f32[1,64]{1,0:T(1,128)S(1)} %get-tuple-element.8.home_ref, bf16[2,512,1024]{2,1,0:T(8,128)(2,1)S(1)} %bitcast.4), custom_call_target="tpu_custom_call" | custom-call | tf_op jit(solution)/shard_map/product/pallas_call | solution.py:757
